TPU v7x, 32 devices: a whole 2x2x4 slice. The times are simulated.
32 devices in a mesh: dp: 8 (over z, x), tensor: 4 (over y, core).
Axes of the slice: x: 2, y: 2, z: 4, core: 2. Of those that a mesh axis runs over, the one named last changes fastest.
Arguments:
- block_input: bfloat16 [8192, 1536], P(('dp', 'tensor')), may hold values from -6 to 6
- gain_attention: float32 [1536], replicated, may hold values from 0.1 to 1.9
- gain_feedforward: float32 [1536], replicated, may hold values from 0.1 to 1.9
- w_query: bfloat16 [1536, 1536], P(None, 'tensor'), as said below
- w_key: bfloat16 [1536, 768], P(None, 'tensor'), as said below
- w_value: bfloat16 [1536, 768], P(None, 'tensor'), may hold values from -0.15625 to 0.15625
- w_output: bfloat16 [1536, 1536], P('tensor'), may hold values from -1.25 to 1.25
- w_gate: bfloat16 [1536, 4096], P(None, 'tensor'), may hold values from -0.15625 to 0.15625
- w_up: bfloat16 [1536, 4096], P(None, 'tensor'), may hold values from -0.15625 to 0.15625
- w_down: bfloat16 [4096, 1536], P('tensor'), may hold values from -0.09375 to 0.09375
- cotangent: bfloat16 [8192, 1536], P(('dp', 'tensor')), may hold values from -12 to 12
Outputs:
- block_output: bfloat16 [8192, 1536], P(('dp', 'tensor'))
- input_grad: bfloat16 [8192, 1536], P(('dp', 'tensor'))
- grad_gain_attention: float32 [1536], replicated
- grad_gain_feedforward: float32 [1536], replicated
- grad_query: float32 [1536, 1536], P(None, 'tensor')
- grad_key: float32 [1536, 768], P(None, 'tensor')
- grad_value: float32 [1536, 768], P(None, 'tensor')
- grad_output: float32 [1536, 1536], P('tensor')
- grad_gate: float32 [1536, 4096], P(None, 'tensor')
- grad_up: float32 [1536, 4096], P(None, 'tensor')
- grad_down: float32 [4096, 1536], P('tensor')
Inputs may be any that keep to these rules, and one draw needn't show every extreme that they name: `w_query`: query projection. `w_key`: key projection with entries of order 1536^-0.5.
All inputs are finite; a program needn't handle non-finite values.
Results may differ from a plain program's by a relative error of at most 0.02.
Values may be sent and summed in bfloat16 or wider, within the bound.
No kernel may reach another device: no remote copies, remote signals or barrier semaphores. Data moves between devices by JAX's collectives and lax.ppermute only.
A program may use at most 192 MiB of HBM per device.

v0:
```python
import jax
import jax.numpy as jnp
from jax import lax
from jax.sharding import PartitionSpec as P

HD = 96
L = 1024
EPS = 1e-05
THETA = 100000.0


def rope_tables(length, width):
    position = jnp.arange(length, dtype=jnp.float32)[:, None]
    inverse = THETA ** (-jnp.arange(0, width, 2, dtype=jnp.float32) / width)
    angles = position * inverse[None, :]
    angles = jnp.concatenate([angles, angles], axis=-1)
    return (jnp.cos(angles), jnp.sin(angles))


def rotate(values_in, cosine, sine):
    half_width = values_in.shape[-1] // 2
    turned = jnp.concatenate([-values_in[..., half_width:], values_in[..., :half_width]], axis=-1)
    return values_in * cosine[:, None, :] + turned * sine[:, None, :]


def unrotate(grad_in, cosine, sine):
    half_width = grad_in.shape[-1] // 2
    scaled = grad_in * sine[:, None, :]
    turned = jnp.concatenate([scaled[..., half_width:], -scaled[..., :half_width]], axis=-1)
    return grad_in * cosine[:, None, :] + turned


def norm_forward(inputs, gain):
    recip = lax.rsqrt(jnp.mean(inputs * inputs, axis=-1, keepdims=True) + EPS)
    return ((inputs * recip * gain).astype(jnp.bfloat16), recip)


def norm_backward(inputs, recip, gain, dnormed):
    scaled = gain * dnormed
    gain_part = jnp.sum(dnormed * inputs * recip, axis=0)
    inner = jnp.mean(scaled * inputs, axis=-1, keepdims=True)
    return (gain_part, recip * scaled - inputs * recip * recip * recip * inner)


def outer_sum(left, right):
    return lax.dot_general(
        left, right, (((0,), (0,)), ((), ())), preferred_element_type=jnp.float32
    )


def times_transpose(left, weight):
    return lax.dot_general(
        left, weight, (((1,), (1,)), ((), ())), preferred_element_type=jnp.float32
    )


def masked_scores(query, keys):
    length = query.shape[0]
    scores = jnp.einsum("lkgd,mkd->kglm", query, keys, preferred_element_type=jnp.float32) * HD ** (
        -0.5
    )
    causal = lax.broadcasted_iota(jnp.int32, (length, length), 0) >= lax.broadcasted_iota(
        jnp.int32, (length, length), 1
    )
    return jnp.where(causal, scores, -jnp.inf)


def attend(query, keys, values):
    scores = masked_scores(query, keys)
    row_max = jnp.max(scores, axis=-1, keepdims=True)
    exponent = jnp.exp(scores - row_max)
    row_total = jnp.sum(exponent, axis=-1, keepdims=True)
    probability = (exponent / row_total).astype(jnp.bfloat16)
    log_total = row_max + jnp.log(row_total)
    attended = jnp.einsum("kglm,mkd->lkgd", probability, values, preferred_element_type=jnp.float32)
    return (attended.astype(jnp.bfloat16), log_total)


def attend_back(query, keys, values, attended, log_total, dattended):
    scores = masked_scores(query, keys)
    probability = jnp.exp(scores - log_total)
    prob_rounded = probability.astype(jnp.bfloat16)
    value_grad = jnp.einsum(
        "kglm,lkgd->mkd", prob_rounded, dattended, preferred_element_type=jnp.float32
    )
    dprob = jnp.einsum("lkgd,mkd->kglm", dattended, values, preferred_element_type=jnp.float32)
    delta = jnp.sum(dattended.astype(jnp.float32) * attended.astype(jnp.float32), axis=-1)
    delta = jnp.transpose(delta, (1, 2, 0))[..., None]
    dscore = (probability * (dprob - delta)).astype(jnp.bfloat16)
    query_grad = jnp.einsum(
        "kglm,mkd->lkgd", dscore, keys, preferred_element_type=jnp.float32
    ) * HD ** (-0.5)
    key_grad = jnp.einsum(
        "kglm,lkgd->mkd", dscore, query, preferred_element_type=jnp.float32
    ) * HD ** (-0.5)
    return (query_grad, key_grad, value_grad)


def body(
    block_input,
    gain_attention,
    gain_feedforward,
    w_query,
    w_key,
    w_value,
    w_output,
    w_gate,
    w_up,
    w_down,
    cotangent,
):
    query_cols = w_query.shape[1]
    pair_cols = w_key.shape[1]
    query_heads = query_cols // HD
    pair_heads = pair_cols // HD
    inputs = block_input.astype(jnp.float32)
    normed_one, recip_one = norm_forward(inputs, gain_attention)
    full_one = lax.all_gather(normed_one, "tensor", axis=0, tiled=True)
    rows_all = full_one.shape[0]
    sequences = rows_all // L
    cosine, sine = rope_tables(L, HD)
    query = jnp.dot(full_one, w_query, preferred_element_type=jnp.float32).reshape(
        sequences, L, query_heads, HD
    )
    query = (
        rotate(query, cosine, sine).astype(jnp.bfloat16).reshape(sequences, L, pair_heads, 2, HD)
    )
    keys = jnp.dot(full_one, w_key, preferred_element_type=jnp.float32).reshape(
        sequences, L, pair_heads, HD
    )
    keys = rotate(keys, cosine, sine).astype(jnp.bfloat16)
    values = (
        jnp.dot(full_one, w_value, preferred_element_type=jnp.float32)
        .astype(jnp.bfloat16)
        .reshape(sequences, L, pair_heads, HD)
    )
    attended, log_total = lax.map(
        lambda members: attend(members[0], members[1], members[2]), (query, keys, values)
    )
    flat_attended = attended.reshape(rows_all, query_cols)
    resid = inputs + lax.psum_scatter(
        jnp.dot(flat_attended, w_output, preferred_element_type=jnp.float32).astype(jnp.bfloat16),
        "tensor",
        scatter_dimension=0,
        tiled=True,
    ).astype(jnp.float32)
    normed_two, recip_two = norm_forward(resid, gain_feedforward)
    full_two = lax.all_gather(normed_two, "tensor", axis=0, tiled=True)
    gate = jnp.dot(full_two, w_gate, preferred_element_type=jnp.float32)
    up_proj = jnp.dot(full_two, w_up, preferred_element_type=jnp.float32)
    sigmoid_gate = jax.nn.sigmoid(gate)
    activated = gate * sigmoid_gate
    hidden = (activated * up_proj).astype(jnp.bfloat16)
    block_output = (
        resid
        + lax.psum_scatter(
            jnp.dot(hidden, w_down, preferred_element_type=jnp.float32).astype(jnp.bfloat16),
            "tensor",
            scatter_dimension=0,
            tiled=True,
        ).astype(jnp.float32)
    ).astype(jnp.bfloat16)
    full_grad = lax.all_gather(cotangent, "tensor", axis=0, tiled=True)
    grad_down = outer_sum(hidden, full_grad)
    dhidden = times_transpose(full_grad, w_down)
    dgate = (dhidden * up_proj * sigmoid_gate * (1.0 + gate * (1.0 - sigmoid_gate))).astype(
        jnp.bfloat16
    )
    dup_proj = (dhidden * activated).astype(jnp.bfloat16)
    grad_gate = outer_sum(full_two, dgate)
    grad_up = outer_sum(full_two, dup_proj)
    dnormed_two = lax.psum_scatter(
        (times_transpose(dgate, w_gate) + times_transpose(dup_proj, w_up)).astype(jnp.bfloat16),
        "tensor",
        scatter_dimension=0,
        tiled=True,
    ).astype(jnp.float32)
    gain_two_part, dresid_norm = norm_backward(resid, recip_two, gain_feedforward, dnormed_two)
    dresid = cotangent.astype(jnp.float32) + dresid_norm
    full_dresid = lax.all_gather(dresid.astype(jnp.bfloat16), "tensor", axis=0, tiled=True)
    grad_output = outer_sum(flat_attended, full_dresid)
    dattended = (
        times_transpose(full_dresid, w_output)
        .astype(jnp.bfloat16)
        .reshape(sequences, L, pair_heads, 2, HD)
    )
    query_grad, key_grad, value_grad = lax.map(
        lambda members: attend_back(
            members[0], members[1], members[2], members[3], members[4], members[5]
        ),
        (query, keys, values, attended, log_total, dattended),
    )
    query_grad = (
        unrotate(query_grad.reshape(sequences, L, query_heads, HD), cosine, sine)
        .astype(jnp.bfloat16)
        .reshape(rows_all, query_cols)
    )
    key_grad = unrotate(key_grad, cosine, sine).astype(jnp.bfloat16).reshape(rows_all, pair_cols)
    value_grad = value_grad.astype(jnp.bfloat16).reshape(rows_all, pair_cols)
    grad_query = outer_sum(full_one, query_grad)
    grad_key = outer_sum(full_one, key_grad)
    grad_value = outer_sum(full_one, value_grad)
    term = times_transpose(query_grad, w_query)
    term = term + times_transpose(key_grad, w_key)
    dnormed_one = lax.psum_scatter(
        (term + times_transpose(value_grad, w_value)).astype(jnp.bfloat16),
        "tensor",
        scatter_dimension=0,
        tiled=True,
    ).astype(jnp.float32)
    gain_one_part, dinput_norm = norm_backward(inputs, recip_one, gain_attention, dnormed_one)
    input_grad = (dresid + dinput_norm).astype(jnp.bfloat16)
    grad_gain_one, grad_gain_two = lax.psum((gain_one_part, gain_two_part), ("dp", "tensor"))
    grad_output, grad_query, grad_key, grad_value, grad_gate, grad_up, grad_down = (
        lax.psum(grad_output.astype(jnp.bfloat16), "dp").astype(jnp.float32),
        lax.psum(grad_query.astype(jnp.bfloat16), "dp").astype(jnp.float32),
        lax.psum(grad_key.astype(jnp.bfloat16), "dp").astype(jnp.float32),
        lax.psum(grad_value.astype(jnp.bfloat16), "dp").astype(jnp.float32),
        lax.psum(grad_gate.astype(jnp.bfloat16), "dp").astype(jnp.float32),
        lax.psum(grad_up.astype(jnp.bfloat16), "dp").astype(jnp.float32),
        lax.psum(grad_down.astype(jnp.bfloat16), "dp").astype(jnp.float32),
    )
    return (
        block_output,
        input_grad,
        grad_gain_one,
        grad_gain_two,
        grad_query,
        grad_key,
        grad_value,
        grad_output,
        grad_gate,
        grad_up,
        grad_down,
    )


def solution(mesh):
    placed = (
        P(("dp", "tensor"), None),
        P(),
        P(),
        P(None, "tensor"),
        P(None, "tensor"),
        P(None, "tensor"),
        P("tensor", None),
        P(None, "tensor"),
        P(None, "tensor"),
        P("tensor", None),
        P(("dp", "tensor"), None),
    )
    return jax.shard_map(
        body,
        mesh=mesh,
        in_specs=placed,
        out_specs=(
            P(("dp", "tensor"), None),
            P(("dp", "tensor"), None),
            P(),
            P(),
            P(None, "tensor"),
            P(None, "tensor"),
            P(None, "tensor"),
            P("tensor", None),
            P(None, "tensor"),
            P(None, "tensor"),
            P("tensor", None),
        ),
        check_vma=False,
    )
```

profile of v0, /device:TPU:0, one launch (start us, length us, event | category | flops | bytes accessed | tf_op | source)
XLA Modules:
  0.0 811.2 jit_solution(7775134368866438504)
XLA Ops:
  15.3 27.7 %all-gather.5.cloned.1.call-done = bf16[1024,1536]{1,0:T(8,128)(2,1)} async-done(((bf16[256,1536]{1,0:T(8,128)(2,1)}), bf16[1024,1536]{1,0:T(8,128)(2,1)}) %all-gather.5.cloned.1.call-update) | async-done | bytes 3145744 | tf_op jit(solution)/shard_map/all_gather | solution.py:118
  53.4 3.7 fusion.2
  59.2 5.1 fusion.34
  68.9 37.8 %reduce-scatter.5.cloned.1.call-done = bf16[256,1536]{1,0:T(8,128)(2,1)} async-done(((bf16[1024,1536]{1,0:T(8,128)(2,1)}), bf16[256,1536]{1,0:T(8,128)(2,1)}) %reduce-scatter.5.cloned.1.call-update) | async-done | bytes 786448 | tf_op jit(solution)/shard_map/reduce_scatter | solution.py:141
  112.2 28.0 %all-gather.7.cloned.1.call-done = bf16[1024,1536]{1,0:T(8,128)(2,1)} async-done(((bf16[256,1536]{1,0:T(8,128)(2,1)}), bf16[1024,1536]{1,0:T(8,128)(2,1)}) %all-gather.7.cloned.1.call-update) | async-done | bytes 3145744 | tf_op jit(solution)/shard_map/all_gather | solution.py:148
  140.3 8.4 %fusion.58 = f32[1024,1024]{1,0:T(8,128)} fusion(bf16[1024,1536]{1,0:T(8,128)(2,1)} %all-gather.7.cloned.1.call-done, bf16[1536,1024]{1,0:T(8,128)(2,1)} %param.19), kind=kOutput, calls=%fused_computation.113 | convolution fusion | flops 3221225472 | bytes 10485760 | tf_op jit(solution)/shard_map/dot_general | solution.py:150
  148.7 4.9 fusion.57
  153.6 16.6 %all-gather.9.cloned.1.call-done = bf16[1024,1536]{1,0:T(8,128)(2,1)} async-done(((bf16[256,1536]{1,0:T(8,128)(2,1)}), bf16[1024,1536]{1,0:T(8,128)(2,1)}) %all-gather.9.cloned.1.call-update) | async-done | bytes 3145744 | tf_op jit(solution)/shard_map/all_gather | solution.py:163
  170.2 9.5 %multiply_convert_fusion = (bf16[1024,1024]{1,0:T(8,128)(2,1)S(1)}, bf16[1024,1024]{1,0:T(8,128)(2,1)S(1)}, bf16[1024,1024]{1,0:T(8,128)(2,1)}) fusion(f32[1024,1024]{1,0:T(8,128)} %fusion.57, f32[1024,1024]{1,0:T(8,128)} %fusion.58, bf16[1024,1536]{1,0:T(8,128)(2,1)} %all-gather.9.cloned.1.call-done, bf16[1024,1536]{1,0:T(8,128)(2,1)S(1)} %copy-done), kind=kOutput, calls=%fused_computation.15 | convolution fusion | flops 3236954112 | bytes 20971520 | tf_op jit(solution)/shard_map/dot_general | solution.py:52
  183.3 4.9 add_convert_fusion.1
  188.2 38.0 %reduce-scatter.9.cloned.1.call-done = bf16[256,1536]{1,0:T(8,128)(2,1)} async-done(((bf16[1024,1536]{1,0:T(8,128)(2,1)}), bf16[256,1536]{1,0:T(8,128)(2,1)}) %reduce-scatter.9.cloned.1.call-update) | async-done | bytes 786448 | tf_op jit(solution)/shard_map/reduce_scatter | solution.py:172
  234.2 26.9 %all-gather.11.cloned.1.call-done = bf16[1024,1536]{1,0:T(8,128)(2,1)} async-done(((bf16[256,1536]{1,0:T(8,128)(2,1)}), bf16[1024,1536]{1,0:T(8,128)(2,1)}) %all-gather.11.cloned.1.call-update) | async-done | bytes 3145744 | tf_op jit(solution)/shard_map/all_gather | solution.py:180
  261.1 3.8 convolution_convert_fusion.9
  265.2 8.2 %fusion.38 = bf16[2,96,1024]{2,1,0:T(8,128)(2,1)S(1)} fusion(bf16[1024,2,2,96]{0,3,2,1:T(8,128)(2,1)S(1)} %bitcast.151, f32[2,1024,1024,2]{2,1,3,0:T(8,128)} %copy-done.1, f32[2,2,1024]{2,1,0:T(2,128)S(1)} %copy-done.38, pred[1024,1024]{0,1:T(8,128)(4,1)S(1)} %copy-done.7), kind=kOutput, calls=%fused_computation.76 | convolution fusion | flops 822280192 | bytes 19021824 | tf_op jit(solution)/shard_map/while/body/eval_jaxpr/kglm,lkgd->mkd/dot_general | solution.py:83
  273.4 9.5 %fusion.1 = bf16[2,2,1024,1024]{2,3,1,0:T(8,128)(2,1)S(1)} fusion(f32[2,1024,1024,2]{2,1,3,0:T(8,128)} %copy-done.1, f32[2,2,1024]{2,1,0:T(2,128)S(1)} %bitcast.153, f32[2,2,1024]{2,1,0:T(2,128)S(1)} %copy-done.38, pred[1024,1024]{0,1:T(8,128)(4,1)S(1)} %copy-done.7, bf16[1024,2,96,1]{0,2,3,1:T(8,128)(2,1)S(1)} %bitcast.155, ...), kind=kOutput, calls=%fused_computation.2 | convolution fusion | flops 830472192 | bytes 27426816 | tf_op jit(solution)/shard_map/while/body/eval_jaxpr/lkgd,mkd->kglm/dot_general | solution.py:86
  295.8 6.4 convolution_convert_fusion.4
  302.4 8.6 %convolution_convert_fusion.1 = bf16[1024,1536]{1,0:T(8,128)(2,1)} fusion(bf16[1024,1024]{1,0:T(8,128)(2,1)} %get-tuple-element.74, bf16[1024,1536]{1,0:T(8,128)(2,1)} %all-gather.9.cloned.1.call-done), kind=kOutput, calls=%fused_computation.22 | convolution fusion | flops 3222798336 | bytes 8388608 | tf_op jit(solution)/shard_map/dot_general | solution.py:46
  311.0 4.9 convolution_convert_fusion.2
  315.9 4.8 convolution_convert_fusion.3
  329.3 4.5 reduce-scatter.11.cloned.1.call-done
  335.6 40.0 %all-reduce = (f32[1536]{0:T(1024)}, f32[1536]{0:T(1024)}) all-reduce(f32[1536]{0:T(1024)S(1)} %get-tuple-element.51, f32[1536]{0:T(1024)S(1)} %get-tuple-element.49), channel_id=1, replica_groups=mesh['dp'=8,'tensor'=4] {'dp','tensor'}, use_global_device_ids=true, to_apply=%region_12.13 | all-reduce | flops 3072 | bytes 24576 | tf_op jit(solution)/shard_map/psum | solution.py:213
  375.6 4.9 fusion.20
  380.5 406.2 %all-reduce.4.cloned.1.call-done = (bf16[1536,384]{1,0:T(8,128)(2,1)}, bf16[1536,192]{0,1:T(8,128)(2,1)}, bf16[1536,192]{0,1:T(8,128)(2,1)}, bf16[384,1536]{1,0:...) async-done(((bf16[1536,384]{1,0:T(8,128)(2,1)}, bf16[1536,192]{0,1:T(8,128)(2,1)}, bf16[1536,192]{0,1:T(8,128)(2,1)}, ...) | async-done | bytes 12976144 | tf_op jit(solution)/shard_map/psum | solution.py:216
  800.6 3.6 convert_element_type.204
  (180 shorter events, 79.6 us)
Async XLA Ops:
  7.2 163.0 %copy-start = (bf16[1024,1536]{1,0:T(8,128)(2,1)S(1)}, bf16[1024,1536]{1,0:T(8,128)(2,1)}, u32[]{:S(2)}) copy-start(bf16[1024,1536]{1,0:T(8,128)(2,1)} %param.20) | copy-start | bytes 9437188
  7.2 35.8 %all-gather.5.cloned.1.call-start = ((), (), s32[]{:S(2)}) async-start(), calls=%async_computation.4 | async-start | bytes 3932160 | tf_op jit(solution)/shard_map/all_gather | solution.py:118
  11.6 95.1 %reduce-scatter.5.cloned.1.call-start = ((), (), s32[]{:S(2)}) async-start(), calls=%async_computation.5 | async-start | bytes 3932160 | tf_op jit(solution)/shard_map/reduce_scatter | solution.py:141
  57.1 7.1 copy-start.35
  58.3 6.0 copy-start.50
  59.2 6.0 copy-start.49
  68.7 40.4 %copy-start.32 = (f32[1536]{0:T(1024)S(1)}, f32[1536]{0:T(1024)}, u32[]{:S(2)}) copy-start(f32[1536]{0:T(1024)} %param.13) | copy-start | bytes 18436
  68.7 71.6 %all-gather.7.cloned.1.call-start = ((), (), s32[]{:S(2)}) async-start(), calls=%async_computation.6 | async-start | bytes 3932160 | tf_op jit(solution)/shard_map/all_gather | solution.py:148
  111.6 58.6 %all-gather.9.cloned.1.call-start = ((), (), s32[]{:S(2)}) async-start(), calls=%async_computation.8 | async-start | bytes 3932160 | tf_op jit(solution)/shard_map/all_gather | solution.py:163
  112.2 114.0 %reduce-scatter.9.cloned.1.call-start = ((), (), s32[]{:S(2)}) async-start(), calls=%async_computation.9 | async-start | bytes 3932160 | tf_op jit(solution)/shard_map/reduce_scatter | solution.py:172
  140.3 8.4 %copy-start.43 = (bf16[1536,1024]{1,0:T(8,128)(2,1)S(1)}, bf16[1536,1024]{1,0:T(8,128)(2,1)}, u32[]{:S(2)}) copy-start(bf16[1536,1024]{1,0:T(8,128)(2,1)} %param.18) | copy-start | bytes 9437188
  140.3 8.4 %copy-start.46 = (bf16[1024,1536]{1,0:T(8,128)(2,1)S(1)}, bf16[1024,1536]{1,0:T(8,128)(2,1)}, u32[]{:S(2)}) copy-start(bf16[1024,1536]{1,0:T(8,128)(2,1)} %all-gather.7.cloned.1.call-done) | copy-start | bytes 9437188
  170.2 9.5 %copy-start.44 = (bf16[1536,1024]{1,0:T(8,128)(2,1)S(1)}, bf16[1536,1024]{1,0:T(8,128)(2,1)}, u32[]{:S(2)}) copy-start(bf16[1536,1024]{1,0:T(8,128)(2,1)} %param.18) | copy-start | bytes 9437188
  188.2 72.9 %all-gather.11.cloned.1.call-start = ((), (), s32[]{:S(2)}) async-start(), calls=%async_computation.10 | async-start | bytes 3932160 | tf_op jit(solution)/shard_map/all_gather | solution.py:180
  232.4 101.4 %reduce-scatter.11.cloned.1.call-start = ((), (), s32[]{:S(2)}) async-start(), calls=%async_computation.11 | async-start | bytes 3932160 | tf_op jit(solution)/shard_map/reduce_scatter | solution.py:205
  265.2 8.3 %copy-start.51 = (bf16[1024,192]{0,1:T(8,128)(2,1)S(1)}, bf16[1024,192]{0,1:T(8,128)(2,1)}, u32[]{:S(2)}) copy-start(bf16[1024,192]{0,1:T(8,128)(2,1)} %copy-done.50) | copy-start | bytes 1179652
  273.4 19.5 %copy-start.19 = (bf16[2,96,1024]{2,1,0:T(8,128)(2,1)}, bf16[2,96,1024]{2,1,0:T(8,128)(2,1)S(1)}, u32[]{:S(2)}) copy-start(bf16[2,96,1024]{2,1,0:T(8,128)(2,1)S(1)} %fusion.38) | copy-start | bytes 1179652
  273.4 9.5 %copy-start.11 = (bf16[1024,2,2,96]{0,3,2,1:T(8,128)(2,1)S(1)}, bf16[1024,2,2,96]{0,3,2,1:T(8,128)(2,1)}, u32[]{:S(2)}) copy-start(bf16[1024,2,2,96]{0,3,2,1:T(8,128)(2,1)} %copy-done.10) | copy-start | bytes 2359300
  295.7 79.9 %reduce-scatter.7.cloned.1.call-start = ((), (), s32[]{:S(2)}) async-start(), calls=%async_computation.7 | async-start | bytes 3932160 | tf_op jit(solution)/shard_map/reduce_scatter | solution.py:156
  302.2 484.6 %all-reduce.4.cloned.1.call-start = ((), (), s32[]{:S(2)}) async-start(), calls=%async_computation.12 | async-start | bytes 25952256 | tf_op jit(solution)/shard_map/psum | solution.py:216
  302.4 8.6 %copy-start.47 = (bf16[1024,1536]{1,0:T(8,128)(2,1)S(1)}, bf16[1024,1536]{1,0:T(8,128)(2,1)}, u32[]{:S(2)}) copy-start(bf16[1024,1536]{1,0:T(8,128)(2,1)} %all-gather.7.cloned.1.call-done) | copy-start | bytes 9437188
  302.4 8.6 %copy-start.55 = (bf16[1024,1024]{1,0:T(8,128)(2,1)S(1)}, bf16[1024,1024]{1,0:T(8,128)(2,1)}, u32[]{:S(2)}) copy-start(bf16[1024,1024]{1,0:T(8,128)(2,1)} %copy-done.54) | copy-start | bytes 6291460
  329.3 46.3 %copy-start.37 = (f32[256]{0:T(256)S(1)}, f32[256]{0:T(256)}, u32[]{:S(2)}) copy-start(f32[256]{0:T(256)} %copy-done.36) | copy-start | bytes 3076
  329.3 46.3 %copy-start.42 = (f32[256]{0:T(256)S(1)}, f32[256]{0:T(256)}, u32[]{:S(2)}) copy-start(f32[256]{0:T(256)} %copy-done.41) | copy-start | bytes 3076
  (41 other events, 122.7 us)
Sparse Core Ops, SparseCore 0:
  11.7 31.2 all-gather.4
  68.8 37.8 reduce-scatter.4
  111.7 28.4 all-gather.6
  141.7 28.4 all-gather.8
  188.3 37.8 reduce-scatter.8
  232.5 28.4 all-gather.10
  295.8 37.8 reduce-scatter.10
  336.9 38.2 reduce-scatter.6
  382.0 404.7 all-reduce.3
where the time goes:
time: 820 us; the launch traced here: 811 us
  waiting for transfers between devices  586 us (71%)
  matrix products  113 us (14%)
  other arithmetic  49 us (6%)
  blocking collectives  40 us (5%)
  between operations  14.9 us (2%)
    psum x1, waiting for transfers between devices, body(): lax.psum(grad_query.astype(jnp.bfloat16), 'dp').astype(jnp.float32)  406 us
    psum x1, blocking collectives, body(): lax.psum((gain_one_part, gain_two_part), ('dp', 'tensor'))  40 us
    reduce_scatter x1, waiting for transfers between devices, body(): lax.psum_scatter((times_transpose(dgate, w_gate) + times_transpose(dup_pr...  38 us
    reduce_scatter x1, waiting for transfers between devices, body(): lax.psum_scatter(jnp.dot(flat_attended, w_output, preferred_element_type=...  37.8 us
    all_gather x1, waiting for transfers between devices, body(): full_two = lax.all_gather(normed_two, 'tensor', axis=0, tiled=True)  28 us
    all_gather x1, waiting for transfers between devices, body(): full_one = lax.all_gather(normed_one, 'tensor', axis=0, tiled=True)  27.7 us
    dot_general x7, matrix products, times_transpose(): lax.dot_general(left, weight, (((1,), (1,)), ((), ())), preferred_element...  27.2 us
    all_gather x1, waiting for transfers between devices, body(): lax.all_gather(dresid.astype(jnp.bfloat16), 'tensor', axis=0, tiled=True)  26.9 us
  transfers between devices with their start and end apart: 9, of which 8 were waited for; matrix products, arithmetic and copies ran while one was open for 7% of the time, Pallas kernels for 0%

commit v1 on v0

--- a/solution.py
+++ b/solution.py
@@ -211,9 +211,10 @@
     gain_one_part, dinput_norm = norm_backward(inputs, recip_one, gain_attention, dnormed_one)
     input_grad = (dresid + dinput_norm).astype(jnp.bfloat16)
     grad_gain_one, grad_gain_two = lax.psum((gain_one_part, gain_two_part), ("dp", "tensor"))
+    post_the_entries = lambda block_here: jnp.sum(jax.lax.all_gather(block_here, "dp"), 0)
     grad_output, grad_query, grad_key, grad_value, grad_gate, grad_up, grad_down = (
         lax.psum(grad_output.astype(jnp.bfloat16), "dp").astype(jnp.float32),
-        lax.psum(grad_query.astype(jnp.bfloat16), "dp").astype(jnp.float32),
+        post_the_entries(grad_query.astype(jnp.bfloat16)).astype(jnp.float32),
         lax.psum(grad_key.astype(jnp.bfloat16), "dp").astype(jnp.float32),
         lax.psum(grad_value.astype(jnp.bfloat16), "dp").astype(jnp.float32),
         lax.psum(grad_gate.astype(jnp.bfloat16), "dp").astype(jnp.float32),

time: 820 us -> 908 us (1.11)
  waiting for transfers between devices: 586 us -> 663 us
    all_gather x0 -> x1, waiting for transfers between devices: none -> 122 us  [body(): jax.lax.all_gather(block_here, 'dp')]
    psum x1, waiting for transfers between devices: 406 us -> 364 us  [body(): lax.psum(grad_key.astype(jnp.bfloat16), 'dp').astype(jnp.float32)]
  transfers between devices with their start and end apart: 9 -> 10, of which waited for: 8 -> 9; matrix products, arithmetic and copies ran while one was open for 7% -> 9% of each run, Pallas kernels for 0% -> 0%
where the time goes in v1:
time: 908 us; the launch traced here: 899 us
  waiting for transfers between devices  663 us (73%)
  matrix products  115 us (13%)
  other arithmetic  57.8 us (6%)
  blocking collectives  40 us (4%)
  between operations  15.2 us (2%)
    psum x1, waiting for transfers between devices, body(): lax.psum(grad_key.astype(jnp.bfloat16), 'dp').astype(jnp.float32)  364 us
    all_gather x1, waiting for transfers between devices, body(): jax.lax.all_gather(block_here, 'dp')  122 us
    psum x1, blocking collectives, body(): lax.psum((gain_one_part, gain_two_part), ('dp', 'tensor'))  40 us
    reduce_scatter x1, waiting for transfers between devices, body(): lax.psum_scatter((times_transpose(dgate, w_gate) + times_transpose(dup_pr...  38 us
    reduce_scatter x1, waiting for transfers between devices, body(): lax.psum_scatter(jnp.dot(flat_attended, w_output, preferred_element_type=...  37.8 us
    dot_general x7, matrix products, outer_sum(): lax.dot_general(left, right, (((0,), (0,)), ((), ())), preferred_element_...  29 us
    all_gather x1, waiting for transfers between devices, body(): full_two = lax.all_gather(normed_two, 'tensor', axis=0, tiled=True)  28 us
    all_gather x1, waiting for transfers between devices, body(): full_one = lax.all_gather(normed_one, 'tensor', axis=0, tiled=True)  27.7 us
  transfers between devices with their start and end apart: 10, of which 9 were waited for; matrix products, arithmetic and copies ran while one was open for 9% of the time, Pallas kernels for 0%

profile of v1, /device:TPU:0, one launch (start us, length us, event | category | flops | bytes accessed | tf_op | source)
XLA Modules:
  0.0 899.3 jit_solution(4656881589462226952)
XLA Ops:
  15.3 27.7 %all-gather.7.cloned.1.call-done = bf16[1024,1536]{1,0:T(8,128)(2,1)} async-done(((bf16[256,1536]{1,0:T(8,128)(2,1)}), bf16[1024,1536]{1,0:T(8,128)(2,1)}) %all-gather.7.cloned.1.call-update) | async-done | bytes 3145744 | tf_op jit(solution)/shard_map/all_gather | solution.py:118
  59.2 5.1 fusion.34
  69.0 37.8 %reduce-scatter.5.cloned.1.call-done = bf16[256,1536]{1,0:T(8,128)(2,1)} async-done(((bf16[1024,1536]{1,0:T(8,128)(2,1)}), bf16[256,1536]{1,0:T(8,128)(2,1)}) %reduce-scatter.5.cloned.1.call-update) | async-done | bytes 786448 | tf_op jit(solution)/shard_map/reduce_scatter | solution.py:141
  112.2 28.0 %all-gather.9.cloned.1.call-done = bf16[1024,1536]{1,0:T(8,128)(2,1)} async-done(((bf16[256,1536]{1,0:T(8,128)(2,1)}), bf16[1024,1536]{1,0:T(8,128)(2,1)}) %all-gather.9.cloned.1.call-update) | async-done | bytes 3145744 | tf_op jit(solution)/shard_map/all_gather | solution.py:148
  140.2 8.4 fusion.58
  148.6 4.9 fusion.57
  153.5 16.6 %all-gather.11.cloned.1.call-done = bf16[1024,1536]{1,0:T(8,128)(2,1)} async-done(((bf16[256,1536]{1,0:T(8,128)(2,1)}), bf16[1024,1536]{1,0:T(8,128)(2,1)}) %all-gather.11.cloned.1.call-update) | async-done | bytes 3145744 | tf_op jit(solution)/shard_map/all_gather | solution.py:163
  170.2 9.5 %multiply_convert_fusion = (bf16[1024,1024]{1,0:T(8,128)(2,1)S(1)}, bf16[1024,1024]{1,0:T(8,128)(2,1)S(1)}, bf16[1024,1024]{1,0:T(8,128)(2,1)}) fusion(f32[1024,1024]{1,0:T(8,128)} %fusion.57, f32[1024,1024]{1,0:T(8,128)} %fusion.58, bf16[1024,1536]{1,0:T(8,128)(2,1)} %all-gather.11.cloned.1.call-done, bf16[1024,1536]{1,0:T(8,128)(2,1)S(1)} %copy-done), kind=kOutput, calls=%fused_computation.15 | convolution fusion | flops 3236954112 | bytes 20971520 | tf_op jit(solution)/shard_map/dot_general | solution.py:52
  183.2 4.9 add_convert_fusion.1
  188.2 38.0 %reduce-scatter.9.cloned.1.call-done = bf16[256,1536]{1,0:T(8,128)(2,1)} async-done(((bf16[1024,1536]{1,0:T(8,128)(2,1)}), bf16[256,1536]{1,0:T(8,128)(2,1)}) %reduce-scatter.9.cloned.1.call-update) | async-done | bytes 786448 | tf_op jit(solution)/shard_map/reduce_scatter | solution.py:172
  234.2 26.9 %all-gather.13.cloned.1.call-done = bf16[1024,1536]{1,0:T(8,128)(2,1)} async-done(((bf16[256,1536]{1,0:T(8,128)(2,1)}), bf16[1024,1536]{1,0:T(8,128)(2,1)}) %all-gather.13.cloned.1.call-update) | async-done | bytes 3145744 | tf_op jit(solution)/shard_map/all_gather | solution.py:180
  265.2 8.2 fusion.38
  273.5 9.5 %fusion.1 = bf16[2,2,1024,1024]{2,3,1,0:T(8,128)(2,1)S(1)} fusion(f32[2,1024,1024,2]{2,1,3,0:T(8,128)} %copy-done.1, f32[2,2,1024]{2,1,0:T(2,128)S(1)} %bitcast.155, f32[2,2,1024]{2,1,0:T(2,128)S(1)} %copy-done.35, pred[1024,1024]{0,1:T(8,128)(4,1)S(1)} %copy-done.7, bf16[1024,2,96,1]{0,2,3,1:T(8,128)(2,1)S(1)} %bitcast.157, ...), kind=kOutput, calls=%fused_computation.2 | convolution fusion | flops 830472192 | bytes 27426816 | tf_op jit(solution)/shard_map/while/body/eval_jaxpr/lkgd,mkd->kglm/dot_general | solution.py:86
  295.8 6.4 convolution_convert_fusion.4
  302.5 8.7 convolution_convert_fusion.1
  311.1 4.9 convolution_convert_fusion.2
  316.0 4.8 convolution_convert_fusion.3
  326.6 4.9 convolution_convert_fusion.6
  335.6 40.0 %all-reduce = (f32[1536]{0:T(1024)}, f32[1536]{0:T(1024)}) all-reduce(f32[1536]{0:T(1024)S(1)} %get-tuple-element.51, f32[1536]{0:T(1024)S(1)} %get-tuple-element.49), channel_id=1, replica_groups=mesh['dp'=8,'tensor'=4] {'dp','tensor'}, use_global_device_ids=true, to_apply=%region_12.13 | all-reduce | flops 3072 | bytes 24576 | tf_op jit(solution)/shard_map/psum | solution.py:213
  375.6 4.9 fusion.20
  380.5 363.5 %all-reduce.4.cloned.1.call-done = (bf16[1536,192]{0,1:T(8,128)(2,1)}, bf16[1536,192]{0,1:T(8,128)(2,1)}, bf16[384,1536]{1,0:T(8,128)(2,1)}, bf16[1536,1024]{1,0...) async-done(((bf16[1536,192]{0,1:T(8,128)(2,1)}, bf16[1536,192]{0,1:T(8,128)(2,1)}, bf16[384,1536]{1,0:T(8,128)(2,1)}, bf16[1536,1024]{1,0:T(8,128)(2,1)}, ...) | async-done | bytes 11796496 | tf_op jit(solution)/shard_map/psum | solution.py:218
  750.3 3.8 convert_element_type.202
  761.2 121.7 %all-gather.15.cloned.1.call-done = bf16[12288,384]{1,0:T(8,128)(2,1)} async-done(((bf16[1536,384]{1,0:T(8,128)(2,1)}), bf16[12288,384]{1,0:T(8,128)(2,1)}) %all-gather.15.cloned.1.call-update) | async-done | bytes 9437200 | tf_op jit(solution)/shard_map/all_gather | solution.py:214
  882.9 6.3 reduce_sum.94
  (178 shorter events, 88.6 us)
Async XLA Ops:
  7.2 163.0 %copy-start = (bf16[1024,1536]{1,0:T(8,128)(2,1)S(1)}, bf16[1024,1536]{1,0:T(8,128)(2,1)}, u32[]{:S(2)}) copy-start(bf16[1024,1536]{1,0:T(8,128)(2,1)} %param.20) | copy-start | bytes 9437188
  7.2 35.8 %all-gather.7.cloned.1.call-start = ((), (), s32[]{:S(2)}) async-start(), calls=%async_computation.4 | async-start | bytes 3932160 | tf_op jit(solution)/shard_map/all_gather | solution.py:118
  11.6 95.1 %reduce-scatter.5.cloned.1.call-start = ((), (), s32[]{:S(2)}) async-start(), calls=%async_computation.5 | async-start | bytes 3932160 | tf_op jit(solution)/shard_map/reduce_scatter | solution.py:141
  68.7 40.3 %copy-start.29 = (f32[1536]{0:T(1024)S(1)}, f32[1536]{0:T(1024)}, u32[]{:S(2)}) copy-start(f32[1536]{0:T(1024)} %param.13) | copy-start | bytes 18436
  68.7 71.5 %all-gather.9.cloned.1.call-start = ((), (), s32[]{:S(2)}) async-start(), calls=%async_computation.6 | async-start | bytes 3932160 | tf_op jit(solution)/shard_map/all_gather | solution.py:148
  111.5 58.6 %all-gather.11.cloned.1.call-start = ((), (), s32[]{:S(2)}) async-start(), calls=%async_computation.8 | async-start | bytes 3932160 | tf_op jit(solution)/shard_map/all_gather | solution.py:163
  112.1 114.0 %reduce-scatter.9.cloned.1.call-start = ((), (), s32[]{:S(2)}) async-start(), calls=%async_computation.9 | async-start | bytes 3932160 | tf_op jit(solution)/shard_map/reduce_scatter | solution.py:172
  140.2 8.4 copy-start.40
  140.2 8.4 copy-start.43
  170.2 9.5 %copy-start.41 = (bf16[1536,1024]{1,0:T(8,128)(2,1)S(1)}, bf16[1536,1024]{1,0:T(8,128)(2,1)}, u32[]{:S(2)}) copy-start(bf16[1536,1024]{1,0:T(8,128)(2,1)} %param.18) | copy-start | bytes 9437188
  188.1 73.0 %all-gather.13.cloned.1.call-start = ((), (), s32[]{:S(2)}) async-start(), calls=%async_computation.10 | async-start | bytes 3932160 | tf_op jit(solution)/shard_map/all_gather | solution.py:180
  232.4 101.4 %reduce-scatter.11.cloned.1.call-start = ((), (), s32[]{:S(2)}) async-start(), calls=%async_computation.11 | async-start | bytes 3932160 | tf_op jit(solution)/shard_map/reduce_scatter | solution.py:205
  265.2 8.3 copy-start.48
  273.4 19.5 %copy-start.18 = (bf16[2,96,1024]{2,1,0:T(8,128)(2,1)}, bf16[2,96,1024]{2,1,0:T(8,128)(2,1)S(1)}, u32[]{:S(2)}) copy-start(bf16[2,96,1024]{2,1,0:T(8,128)(2,1)S(1)} %fusion.38) | copy-start | bytes 1179652
  273.4 9.5 %copy-start.10 = (bf16[1024,2,2,96]{0,3,2,1:T(8,128)(2,1)S(1)}, bf16[1024,2,2,96]{0,3,2,1:T(8,128)(2,1)}, u32[]{:S(2)}) copy-start(bf16[1024,2,2,96]{0,3,2,1:T(8,128)(2,1)} %copy-done.9) | copy-start | bytes 2359300
  295.7 79.9 %reduce-scatter.7.cloned.1.call-start = ((), (), s32[]{:S(2)}) async-start(), calls=%async_computation.7 | async-start | bytes 3932160 | tf_op jit(solution)/shard_map/reduce_scatter | solution.py:156
  302.2 441.9 %all-reduce.4.cloned.1.call-start = ((), (), s32[]{:S(2)}) async-start(), calls=%async_computation.13 | async-start | bytes 23592960 | tf_op jit(solution)/shard_map/psum | solution.py:218
  302.4 8.7 copy-start.44
  302.4 8.7 copy-start.52
  326.5 7.2 copy-start.30
  326.6 7.2 copy-start.37
  326.6 49.0 %copy-start.34 = (f32[256]{0:T(256)S(1)}, f32[256]{0:T(256)}, u32[]{:S(2)}) copy-start(f32[256]{0:T(256)} %copy-done.33) | copy-start | bytes 3076
  326.6 49.0 %copy-start.39 = (f32[256]{0:T(256)S(1)}, f32[256]{0:T(256)}, u32[]{:S(2)}) copy-start(f32[256]{0:T(256)} %copy-done.38) | copy-start | bytes 3076
  326.6 556.3 %all-gather.15.cloned.1.call-start = ((), (), s32[]{:S(2)}) async-start(), calls=%async_computation.12 | async-start | bytes 10616832 | tf_op jit(solution)/shard_map/all_gather | solution.py:214
  (39 other events, 125.1 us)
Sparse Core Ops, SparseCore 0:
  11.7 31.2 all-gather.6
  68.8 37.8 reduce-scatter.4
  111.7 28.4 all-gather.8
  141.6 28.4 all-gather.10
  188.2 37.8 reduce-scatter.8
  232.5 28.5 all-gather.12
  295.8 37.8 reduce-scatter.10
  336.9 38.2 reduce-scatter.6
  381.5 362.4 all-reduce.3
  746.7 136.1 all-gather.14
